TPU v7x, 128 devices: a whole 4x4x4 slice. The times are simulated.
128 devices in a mesh: rows: 32 (over x, y, core), grp: 4 (over z).
Axes of the slice: x: 4, y: 4, z: 4, core: 2. Of those that a mesh axis runs over, the one named last changes fastest.
Arguments:
- embeddings: bfloat16 [262144, 1024], P('rows', 'grp'), may hold values from -6 to 6
- fine_local: int32 [262144], P('rows'), may hold values from 0 to 2047
- send_counts: int32 [32, 32], P('rows'), may hold values from 0 to 512, as said below
- old_fine: bfloat16 [65536, 1024], P('rows', 'grp'), may hold values from -6 to 6
- coarse_ids: int32 [65536], P('rows'), may hold values from 0 to 8191, as said below
- old_coarse: bfloat16 [8192, 1024], P('rows', 'grp'), may hold values from -6 to 6
Outputs:
- new_fine: bfloat16 [65536, 1024], P('rows', 'grp')
- coarse_dirs: bfloat16 [8192, 1024], P('rows')
Inputs may be any that keep to these rules, and one draw needn't show every extreme that they name: Row d of send_counts splits the 8192 rows of block d, in order, into segments for owners 0, 1, ...; each row of send_counts sums to 8192; one owner receives exactly 512 rows from every block. `coarse_ids`: within each block of 2048 consecutive level-1 clusters, at most 128 have a level-2 cluster in any one block of 256 consecutive level-2 clusters; one such block reaches that from every block.
All inputs are finite; a program needn't handle non-finite values.
Results may differ from a plain program's by a relative error of at most 0.006.
Values may be sent and summed in bfloat16 or wider, within the bound.
No kernel may reach another device: no remote copies, remote signals or barrier semaphores. Data moves between devices by JAX's collectives and lax.ppermute only.
A program may use at most 64 MiB of HBM per device.

v0:
```python
import math

import jax
import jax.numpy as jnp
from jax import lax
from jax.sharding import PartitionSpec as P


def onehot_sums(arrived, arrived_labels, fine_dev):
    slot_total = arrived.shape[0]
    width = arrived.shape[1]
    block_rows = math.gcd(slot_total, 2048)
    block_count = slot_total // block_rows
    cluster_index = jnp.arange(fine_dev, dtype=jnp.int32)

    def accumulate(state_pair, pieces):
        fine_sums, totals = state_pair
        row_block, label_block = pieces
        onehot = cluster_index[:, None] == label_block[None, :]
        fine_sums = fine_sums + jnp.dot(
            onehot.astype(jnp.bfloat16), row_block, preferred_element_type=jnp.float32
        )
        totals = totals + jnp.sum(onehot.astype(jnp.int32), axis=1)
        return ((fine_sums, totals), None)

    start_state = (jnp.zeros((fine_dev, width), jnp.float32), jnp.zeros((fine_dev,), jnp.int32))
    (fine_sums, totals), _ = lax.scan(
        accumulate,
        start_state,
        (
            arrived.reshape(block_count, block_rows, width),
            arrived_labels.reshape(block_count, block_rows),
        ),
    )
    return (fine_sums, totals.astype(jnp.float32))


def on_device(embeddings, fine_local, send_counts, old_fine, coarse_ids, old_coarse):
    peer_count = lax.axis_size("rows")
    per_dev = embeddings.shape[0]
    quarter = embeddings.shape[1]
    fine_dev = old_fine.shape[0]
    coarse_dev = old_coarse.shape[0]
    capacity = 2 * per_dev // peer_count
    counts = send_counts[0]
    starts = jnp.cumsum(counts) - counts
    offset = jnp.arange(capacity, dtype=jnp.int32)
    is_live = offset[None, :] < counts[:, None]
    padded_rows = jnp.concatenate(
        [embeddings, jnp.zeros((capacity, quarter), jnp.bfloat16)], axis=0
    )
    padded_local = jnp.concatenate([fine_local, jnp.zeros((capacity,), jnp.int32)], axis=0)

    def take_segment(first_row):
        segment_rows = lax.dynamic_slice_in_dim(padded_rows, first_row, capacity, 0)
        segment_labels = lax.dynamic_slice_in_dim(padded_local, first_row, capacity, 0)
        return (segment_rows, segment_labels)

    outgoing, raw_labels = lax.map(take_segment, starts)
    outgoing = jnp.where(is_live[:, :, None], outgoing, jnp.zeros((), jnp.bfloat16))
    labels = jnp.where(is_live, raw_labels, -1)
    arrived, arrived_labels = (
        lax.all_to_all(outgoing, "rows", split_axis=0, concat_axis=0, tiled=True),
        lax.all_to_all(labels, "rows", split_axis=0, concat_axis=0, tiled=True),
    )
    fine_sums, totals = onehot_sums(
        arrived.reshape(-1, quarter), arrived_labels.reshape(-1), fine_dev
    )
    new_fine = ((fine_sums + old_fine.astype(jnp.float32)) / (totals + 1.0)[:, None]).astype(
        jnp.bfloat16
    )
    owners = coarse_ids // coarse_dev
    local_id = coarse_ids - owners * coarse_dev
    capacity_two = 2 * fine_dev // peer_count
    member = (owners[:, None] == jnp.arange(peer_count, dtype=jnp.int32)[None, :]).astype(jnp.int32)
    slot_rank = jnp.sum(jnp.cumsum(member, axis=0) * member, axis=1) - 1
    slot_pos = owners * capacity_two + slot_rank
    placement = (
        jnp.arange(peer_count * capacity_two, dtype=jnp.int32)[:, None] == slot_pos[None, :]
    ).astype(jnp.bfloat16)
    outgoing_two = jnp.dot(placement, new_fine, preferred_element_type=jnp.float32).astype(
        jnp.bfloat16
    )
    label_plus = jnp.dot(
        placement, (local_id + 1).astype(jnp.bfloat16), preferred_element_type=jnp.float32
    )
    labels_two = label_plus.astype(jnp.int32) - 1
    received, received_labels = (
        lax.all_to_all(
            outgoing_two.reshape(peer_count, capacity_two, quarter),
            "rows",
            split_axis=0,
            concat_axis=0,
            tiled=True,
        ),
        lax.all_to_all(
            labels_two.reshape(peer_count, capacity_two),
            "rows",
            split_axis=0,
            concat_axis=0,
            tiled=True,
        ),
    )
    onehot_two = (
        jnp.arange(coarse_dev, dtype=jnp.int32)[:, None] == received_labels.reshape(-1)[None, :]
    )
    coarse_sums = jnp.dot(
        onehot_two.astype(jnp.bfloat16),
        received.reshape(-1, quarter),
        preferred_element_type=jnp.float32,
    )
    coarse_totals = jnp.sum(onehot_two.astype(jnp.int32), axis=1).astype(jnp.float32)
    coarse_means = (coarse_sums + old_coarse.astype(jnp.float32)) / (coarse_totals + 1.0)[:, None]
    full_means = lax.all_gather(coarse_means, "grp", axis=1, tiled=True)
    scale = lax.rsqrt(jnp.mean(full_means * full_means, axis=1, keepdims=True) + 1e-06)
    coarse_dirs = (full_means * scale).astype(jnp.bfloat16)
    return (new_fine, coarse_dirs)


def solution(mesh):
    in_specs = (
        P("rows", "grp"),
        P("rows"),
        P("rows", None),
        P("rows", "grp"),
        P("rows"),
        P("rows", "grp"),
    )
    out_specs = (P("rows", "grp"), P("rows", None))
    return jax.shard_map(
        on_device, mesh=mesh, in_specs=in_specs, out_specs=out_specs, check_vma=False
    )
```

profile of v0, /device:TPU:0, one launch (start us, length us, event | category | flops | bytes accessed | tf_op | source)
XLA Modules:
  0.0 446.7 jit_solution(14028012184819032292)
XLA Ops:
  9.5 3.9 concatenate.6
  13.4 147.6 %while.27 = (s32[]{:T(128)}, bf16[32,512,256]{2,1,0:T(8,128)(2,1)}, s32[32,512]{1,0:T(8,128)S(1)}, s32[32]{0:T(128)S(1)}, bf16[8704,256]{1,0:T(8,128)(2,1)}, /*index=5*/s32[8704]{0:T(1024)S(1)}) while((s32[]{:T(128)}, bf16[32,512,256]{2,1,0:T(8,128)(2,1)}, s32[32,512]{1,0:T(8,128)S(1)}, s32[32]{0:T(128)S(1)}, ...), condition=%wide.region_2.3_spmd.clone, body=%wide.region_1.2_spmd.sunk.clone | while | flops 5 | bytes 533119 | solution.py:59
  53.0 1.7 bitcast_dynamic-update-slice_fusion.3
  161.8 7.4 %all-to-all-start = ((s32[32,1,512]{2,1,0:T(1,128)}), s32[32,1,512]{2,1,0:T(1,128)S(1)}, u32[]{:S(2)}, u32[]{:S(2)}) async-start(s32[32,1,512]{2,1,0:T(1,128)} %all_to_all.18), calls=%async_computation | async-start | bytes 131072 | tf_op jit(solution)/shard_map/all_to_all | solution.py:64
  169.3 8.1 %broadcast_select_fusion = bf16[32,512,256]{2,1,0:T(8,128)(2,1)} fusion(bf16[32,512,256]{2,1,0:T(8,128)(2,1)} %get-tuple-element.69, pred[32,512]{1,0:T(8,128)(4,1)S(1)} %iota_compare_fusion.17), kind=kLoop, calls=%fused_computation.18 | loop fusion | flops 4194304 | bytes 16793600 | tf_op jit(solution)/shard_map/jit(_where)/select_n | solution.py:60
  177.4 7.6 %all-to-all-start.1 = ((bf16[32,512,256]{2,1,0:T(8,128)(2,1)}), bf16[32,512,256]{2,1,0:T(8,128)(2,1)}, u32[]{:S(2)}, u32[]{:S(2)}) async-start(bf16[32,512,256]{2,1,0:T(8,128)(2,1)} %broadcast_select_fusion), calls=%async_computation.1 | async-start | bytes 16777216 | tf_op jit(solution)/shard_map/all_to_all | solution.py:63
  185.1 9.1 %reduce-window.20 = s32[32,16,128]{2,1,0:T(8,128)S(1)} reduce-window(s32[32,16,128]{2,1,0:T(8,128)S(1)} %fusion.21, s32[]{:T(128)} %copy.41), window={size=1x1x128 pad=0_0x0_0x127_0}, to_apply=%region_6.7 | reduce-window | flops 8323072 | bytes 524292 | tf_op jit(solution)/shard_map/reduce-window.1
  195.1 5.6 %fusion.11 = f32[1,4096]{1,0:T(1,128)S(1)} fusion(bf16[2048,1]{0,1:T(2,128)(2,1)S(1)} %reshape.106, s32[2048]{0:T(1024)S(1)} %get-tuple-element.115), kind=kOutput, calls=%fused_computation.15 | convolution fusion | flops 25165824 | bytes 28672 | tf_op jit(solution)/shard_map/dot_general | solution.py:84
  201.5 97.1 %all-to-all-done.1 = bf16[32,512,256]{2,1,0:T(8,128)(2,1)} async-done(((bf16[32,512,256]{2,1,0:T(8,128)(2,1)}), bf16[32,512,256]{2,1,0:T(8,128)(2,1)}, u32[]{:S(2)}, u32[]{:S(2)}) %all-to-all-start.1) | async-done | bytes 8388640 | tf_op jit(solution)/shard_map/all_to_all | solution.py:63
  298.6 14.2 %all-to-all-start.2 = ((s32[32,1,128]{2,1,0:T(1,128)}), s32[32,1,128]{2,1,0:T(1,128)S(1)}, u32[]{:S(2)}, u32[]{:S(2)}) async-start(s32[32,1,128]{2,1,0:T(1,128)} %bitcast.11), calls=%async_computation.2 | async-start | bytes 32768 | tf_op jit(solution)/shard_map/all_to_all | solution.py:96
  312.8 54.2 %while.28 = (s32[]{:T(128)}, f32[2048,256]{1,0:T(8,128)S(1)}, s32[2048]{0:T(1024)S(1)}, s32[8,2048]{1,0:T(8,128)S(1)}, bf16[8,2048,256]{2,1,0:T(8,128)(2,1)}) while((s32[]{:T(128)}, f32[2048,256]{1,0:T(8,128)S(1)}, s32[2048]{0:T(1024)S(1)}, s32[8,2048]{1,0:T(8,128)S(1)}, bf16[8,2048,256]{2,1,0:T(8,128)(2,1)}) %tuple.50), condition=%wide.region_5.6_spmd.clone.clone, body=%wide.region_3.5_spmd.clone.sunk.clone | while | flops 2165311488 | bytes 5309004 | solution.py:27
  312.8 5.1 %fusion.35 = f32[2048,256]{1,0:T(8,128)S(1)} fusion(s32[2048]{0:T(1024)S(1)} %bitcast.55, f32[2048,256]{1,0:T(8,128)S(1)} %get-tuple-element.239, bf16[8,2048,256]{2,1,0:T(8,128)(2,1)} %get-tuple-element.247, s32[]{:T(128)} %get-tuple-element.238, pred[]{:T(512)S(6)} %compare.8), kind=kOutput, calls=%fused_computation.7.clone.1.clone | convolution fusion | flops 2152726528 | bytes 5251585 | tf_op jit(solution)/shard_map/while/body/eval_jaxpr/dot_general | solution.py:20
  319.7 5.0 %fusion.35 = f32[2048,256]{1,0:T(8,128)S(1)} fusion(s32[2048]{0:T(1024)S(1)} %bitcast.55, f32[2048,256]{1,0:T(8,128)S(1)} %get-tuple-element.239, bf16[8,2048,256]{2,1,0:T(8,128)(2,1)} %get-tuple-element.247, s32[]{:T(128)} %get-tuple-element.238, pred[]{:T(512)S(6)} %compare.8), kind=kOutput, calls=%fused_computation.7.clone.1.clone | convolution fusion | flops 2152726528 | bytes 5251585 | tf_op jit(solution)/shard_map/while/body/eval_jaxpr/dot_general | solution.py:20
  326.4 5.0 %fusion.35 = f32[2048,256]{1,0:T(8,128)S(1)} fusion(s32[2048]{0:T(1024)S(1)} %bitcast.55, f32[2048,256]{1,0:T(8,128)S(1)} %get-tuple-element.239, bf16[8,2048,256]{2,1,0:T(8,128)(2,1)} %get-tuple-element.247, s32[]{:T(128)} %get-tuple-element.238, pred[]{:T(512)S(6)} %compare.8), kind=kOutput, calls=%fused_computation.7.clone.1.clone | convolution fusion | flops 2152726528 | bytes 5251585 | tf_op jit(solution)/shard_map/while/body/eval_jaxpr/dot_general | solution.py:20
  333.2 5.0 %fusion.35 = f32[2048,256]{1,0:T(8,128)S(1)} fusion(s32[2048]{0:T(1024)S(1)} %bitcast.55, f32[2048,256]{1,0:T(8,128)S(1)} %get-tuple-element.239, bf16[8,2048,256]{2,1,0:T(8,128)(2,1)} %get-tuple-element.247, s32[]{:T(128)} %get-tuple-element.238, pred[]{:T(512)S(6)} %compare.8), kind=kOutput, calls=%fused_computation.7.clone.1.clone | convolution fusion | flops 2152726528 | bytes 5251585 | tf_op jit(solution)/shard_map/while/body/eval_jaxpr/dot_general | solution.py:20
  340.0 5.0 %fusion.35 = f32[2048,256]{1,0:T(8,128)S(1)} fusion(s32[2048]{0:T(1024)S(1)} %bitcast.55, f32[2048,256]{1,0:T(8,128)S(1)} %get-tuple-element.239, bf16[8,2048,256]{2,1,0:T(8,128)(2,1)} %get-tuple-element.247, s32[]{:T(128)} %get-tuple-element.238, pred[]{:T(512)S(6)} %compare.8), kind=kOutput, calls=%fused_computation.7.clone.1.clone | convolution fusion | flops 2152726528 | bytes 5251585 | tf_op jit(solution)/shard_map/while/body/eval_jaxpr/dot_general | solution.py:20
  346.7 5.0 %fusion.35 = f32[2048,256]{1,0:T(8,128)S(1)} fusion(s32[2048]{0:T(1024)S(1)} %bitcast.55, f32[2048,256]{1,0:T(8,128)S(1)} %get-tuple-element.239, bf16[8,2048,256]{2,1,0:T(8,128)(2,1)} %get-tuple-element.247, s32[]{:T(128)} %get-tuple-element.238, pred[]{:T(512)S(6)} %compare.8), kind=kOutput, calls=%fused_computation.7.clone.1.clone | convolution fusion | flops 2152726528 | bytes 5251585 | tf_op jit(solution)/shard_map/while/body/eval_jaxpr/dot_general | solution.py:20
  353.5 5.0 %fusion.35 = f32[2048,256]{1,0:T(8,128)S(1)} fusion(s32[2048]{0:T(1024)S(1)} %bitcast.55, f32[2048,256]{1,0:T(8,128)S(1)} %get-tuple-element.239, bf16[8,2048,256]{2,1,0:T(8,128)(2,1)} %get-tuple-element.247, s32[]{:T(128)} %get-tuple-element.238, pred[]{:T(512)S(6)} %compare.8), kind=kOutput, calls=%fused_computation.7.clone.1.clone | convolution fusion | flops 2152726528 | bytes 5251585 | tf_op jit(solution)/shard_map/while/body/eval_jaxpr/dot_general | solution.py:20
  360.3 5.0 %fusion.35 = f32[2048,256]{1,0:T(8,128)S(1)} fusion(s32[2048]{0:T(1024)S(1)} %bitcast.55, f32[2048,256]{1,0:T(8,128)S(1)} %get-tuple-element.239, bf16[8,2048,256]{2,1,0:T(8,128)(2,1)} %get-tuple-element.247, s32[]{:T(128)} %get-tuple-element.238, pred[]{:T(512)S(6)} %compare.8), kind=kOutput, calls=%fused_computation.7.clone.1.clone | convolution fusion | flops 2152726528 | bytes 5251585 | tf_op jit(solution)/shard_map/while/body/eval_jaxpr/dot_general | solution.py:20
  368.4 7.4 %fusion.14 = bf16[4096,256]{1,0:T(8,128)(2,1)} fusion(bf16[2048,256]{1,0:T(8,128)(2,1)S(1)} %divide_convert_fusion, s32[2048]{0:T(1024)S(1)} %get-tuple-element.115), kind=kOutput, calls=%fused_computation.19 | convolution fusion | flops 4304404480 | bytes 3153920 | tf_op jit(solution)/shard_map/dot_general | solution.py:81
  375.8 7.3 %all-to-all-start.3 = ((bf16[32,128,256]{2,1,0:T(8,128)(2,1)}), bf16[32,128,256]{2,1,0:T(8,128)(2,1)S(1)}, u32[]{:S(2)}, u32[]{:S(2)}) async-start(bf16[32,128,256]{2,1,0:T(8,128)(2,1)} %bitcast.13), calls=%async_computation.3 | async-start | bytes 4194304 | tf_op jit(solution)/shard_map/all_to_all | solution.py:89
  383.7 28.4 %all-to-all-done.3 = bf16[32,128,256]{2,1,0:T(8,128)(2,1)S(1)} async-done(((bf16[32,128,256]{2,1,0:T(8,128)(2,1)}), bf16[32,128,256]{2,1,0:T(8,128)(2,1)S(1)}, u32[]{:S(2)}, u32[]{:S(2)}) %all-to-all-start.3) | async-done | bytes 2097184 | tf_op jit(solution)/shard_map/all_to_all | solution.py:89
  413.6 22.8 %all-gather.2.cloned.1.call-done = f32[256,1024]{1,0:T(8,128)} async-done(((f32[256,256]{1,0:T(8,128)}), f32[256,1024]{1,0:T(8,128)}) %all-gather.2.cloned.1.call-update) | async-done | bytes 1048592 | tf_op jit(solution)/shard_map/all_gather | solution.py:114
  437.7 2.1 multiply_convert_fusion
  (196 shorter events, 102.2 us)
Async XLA Ops:
  9.5 151.5 %copy-start.3 = (s32[1,32]{1,0:T(1,128)S(1)}, s32[1,32]{1,0:T(1,128)}, u32[]{:S(2)}) copy-start(s32[1,32]{1,0:T(1,128)} %param.12) | copy-start | bytes 388
  161.8 15.6 %all-to-all-start = ((s32[32,1,512]{2,1,0:T(1,128)}), s32[32,1,512]{2,1,0:T(1,128)S(1)}, u32[]{:S(2)}, u32[]{:S(2)}) async-start(s32[32,1,512]{2,1,0:T(1,128)} %all_to_all.18), calls=%async_computation | async-start | bytes 131072 | tf_op jit(solution)/shard_map/all_to_all | solution.py:64
  177.4 7.7 %copy-start.2 = (s32[2048]{0:T(1024)S(1)}, s32[2048]{0:T(1024)}, u32[]{:S(2)}) copy-start(s32[2048]{0:T(1024)} %param.14) | copy-start | bytes 24580
  177.4 121.2 %all-to-all-start.1 = ((bf16[32,512,256]{2,1,0:T(8,128)(2,1)}), bf16[32,512,256]{2,1,0:T(8,128)(2,1)}, u32[]{:S(2)}, u32[]{:S(2)}) async-start(bf16[32,512,256]{2,1,0:T(8,128)(2,1)} %broadcast_select_fusion), calls=%async_computation.1 | async-start | bytes 16777216 | tf_op jit(solution)/shard_map/all_to_all | solution.py:63
  298.6 77.3 %all-to-all-start.2 = ((s32[32,1,128]{2,1,0:T(1,128)}), s32[32,1,128]{2,1,0:T(1,128)S(1)}, u32[]{:S(2)}, u32[]{:S(2)}) async-start(s32[32,1,128]{2,1,0:T(1,128)} %bitcast.11), calls=%async_computation.2 | async-start | bytes 32768 | tf_op jit(solution)/shard_map/all_to_all | solution.py:96
  312.8 54.2 %copy-start = (bf16[2048,256]{1,0:T(8,128)(2,1)S(1)}, bf16[2048,256]{1,0:T(8,128)(2,1)}, u32[]{:S(2)}) copy-start(bf16[2048,256]{1,0:T(8,128)(2,1)} %param.13) | copy-start | bytes 3145732
  367.4 1.0 copy-start.1
  375.8 36.3 %copy-start.4 = (bf16[256,256]{1,0:T(8,128)(2,1)S(1)}, bf16[256,256]{1,0:T(8,128)(2,1)}, u32[]{:S(2)}) copy-start(bf16[256,256]{1,0:T(8,128)(2,1)} %param.15) | copy-start | bytes 393220
  375.8 36.3 %all-to-all-start.3 = ((bf16[32,128,256]{2,1,0:T(8,128)(2,1)}), bf16[32,128,256]{2,1,0:T(8,128)(2,1)S(1)}, u32[]{:S(2)}, u32[]{:S(2)}) async-start(bf16[32,128,256]{2,1,0:T(8,128)(2,1)} %bitcast.13), calls=%async_computation.3 | async-start | bytes 4194304 | tf_op jit(solution)/shard_map/all_to_all | solution.py:89
  383.2 53.1 %all-gather.2.cloned.1.call-start = ((), (), s32[]{:S(2)}) async-start(), calls=%async_computation.4 | async-start | bytes 1310720 | tf_op jit(solution)/shard_map/all_gather | solution.py:114
Sparse Core Ops, SparseCore 0:
  413.7 22.5 all-gather.1
where the time goes:
time: 450 us; the launch traced here: 447 us
  waiting for transfers between devices  148 us (33%)
  local copies, waits for them, and re-layouts  87.8 us (20%)
  loops' own time  67.7 us (15%)
  matrix products  54.3 us (12%)
  other arithmetic  37.7 us (8%)
  starting transfers between devices  36.7 us (8%)
  between operations  14.2 us (3%)
    all_to_all x1, waiting for transfers between devices, on_device(): lax.all_to_all(outgoing, 'rows', split_axis=0, concat_axis=0, tiled=True)  97.1 us
    another operation x1, loops' own time, on_device(): outgoing, raw_labels = lax.map(take_segment, starts)  67.3 us
    dynamic_update_slice x64, local copies, waits for them, and re-layouts, on_device(): outgoing, raw_labels = lax.map(take_segment, starts)  56.5 us
    dot_general x8, matrix products, accumulate(): jnp.dot(onehot.astype(jnp.bfloat16), row_block, preferred_element_type=jn...  39.8 us
    all_to_all x1, waiting for transfers between devices, on_device(): lax.all_to_all(outgoing_two.reshape(peer_count, capacity_two, quarter), '...  28.4 us
    all_gather x1, waiting for transfers between devices, on_device(): full_means = lax.all_gather(coarse_means, 'grp', axis=1, tiled=True)  22.8 us
    dynamic_slice x32, local copies, waits for them, and re-layouts, on_device(): outgoing, raw_labels = lax.map(take_segment, starts)  21.4 us
    all_to_all x1, starting transfers between devices, on_device(): lax.all_to_all(labels_two.reshape(peer_count, capacity_two), 'rows', spli...  14.2 us
  transfers between devices with their start and end apart: 5, of which 3 were waited for; matrix products, arithmetic and copies ran while one was open for 19% of the time, Pallas kernels for 0%

commit v1 on v0

v1 whole, which is shorter than its diff:
```python
import functools

import jax
import jax.numpy as jnp
from jax import lax
from jax.experimental import pallas as pl
from jax.experimental.pallas import tpu as pltpu
from jax.sharding import PartitionSpec as P

F32 = jnp.float32
BF16 = jnp.bfloat16
LANES = 128
TAIL = 8
FIRST = 384


def iota(shape, axis):
    return lax.broadcasted_iota(jnp.int32, shape, axis)


def pack_body(lo_row, rows, capacity, counts, emb, local, *rest):
    extra = rest[0] if len(rest) == 4 else None
    out, wide, labels = rest[-3:]
    owner = pl.program_id(0)
    per_dev = emb.shape[0]
    label_rows = local.shape[0]

    @pl.when(owner == 0)
    def _():
        for at in range(0, per_dev, 512):
            wide[at : at + 512, :] = emb[at : at + 512, :].astype(F32)
        wide[per_dev:, :] = jnp.zeros((capacity + 8, emb.shape[1]), F32)
        labels[:label_rows, :] = local[...]
        labels[label_rows:, :] = jnp.zeros((16, LANES), jnp.int32)

    start = lax.fori_loop(0, owner, lambda o, s: s + counts[0, o], 0)
    count = counts[0, owner]
    first = start + lo_row
    aligned = first // 8
    turn = first - aligned * 8
    turn_back = lax.rem(8 - turn, 8)
    kept = iota((8, 8, emb.shape[1]), 1) < 8 - turn
    for at in range(0, rows, 64):
        window = wide[pl.ds(pl.multiple_of(aligned * 8 + at, 8), 72), :]
        window = pltpu.roll(window.reshape(9, 8, emb.shape[1]), turn_back, 1)
        moved = jnp.where(kept, window[:8], window[1:])
        out[0, at : at + 64, :] = moved.reshape(64, emb.shape[1]).astype(BF16)
    base = first // LANES
    shift = first - base * LANES
    lines = [labels[pl.ds(base + i, 1), :] for i in range(TAIL + 1)]
    here = jnp.concatenate(lines[:TAIL], axis=0)
    after = jnp.concatenate(lines[1:], axis=0)
    back = lax.rem(LANES - shift, LANES)
    here = pltpu.roll(here, back, 1)
    after = pltpu.roll(after, back, 1)
    lane = iota((TAIL, LANES), 1)
    value = jnp.where(lane < LANES - shift, here, after)
    place = iota((TAIL, LANES), 0) * LANES + lane + lo_row
    live = place < count
    high = jnp.where(live, value // LANES, 64).astype(F32)
    low = jnp.where(live, value % LANES, 0).astype(F32)
    if extra is not None:
        high = jnp.where(iota((TAIL, LANES), 0) == 1, extra[pl.ds(owner, 1), :], high)
    out[0, rows:, :] = jnp.concatenate([high, low], axis=1).astype(BF16)


def pack(send_counts, embeddings, local, extra, lo_row, rows, capacity):
    per_dev, width = embeddings.shape
    owners = send_counts.shape[1]
    operands = [send_counts, embeddings, local] + ([] if extra is None else [extra])
    specs = [pl.BlockSpec(memory_space=pltpu.SMEM)] + [
        pl.BlockSpec(a.shape, lambda o: (0, 0)) for a in operands[1:]
    ]
    return pl.pallas_call(
        functools.partial(pack_body, lo_row, rows, capacity),
        grid=(owners,),
        out_shape=jax.ShapeDtypeStruct((owners, rows + TAIL, width), BF16),
        in_specs=specs,
        out_specs=pl.BlockSpec((1, rows + TAIL, width), lambda o: (o, 0, 0)),
        scratch_shapes=[
            pltpu.VMEM((per_dev + capacity + 8, width), F32),
            pltpu.VMEM((local.shape[0] + 16, LANES), jnp.int32),
        ],
        name="pack_rows",
    )(*operands)


def accumulate(block, group, rows, digits, acc, counts, onehot):
    tail = block[:, rows:, :].astype(F32)
    high, low = [], []
    for g in range(group):
        for at in range(rows // LANES):
            high.append(tail[g, at : at + 1, :LANES])
            low.append(tail[g, at : at + 1, LANES : 2 * LANES])
    high = jnp.concatenate(high, axis=1)
    low = jnp.concatenate(low, axis=1)
    depth = group * rows
    low_hot = jnp.where(iota((LANES, depth), 0).astype(F32) == low, 1.0, 0.0).astype(BF16)
    high_hot = jnp.where(iota((digits, depth), 0).astype(F32) == high, 1.0, 0.0)
    for h in range(digits):
        row = jnp.broadcast_to(high_hot[h : h + 1, :], (16, depth)).astype(BF16)
        for at in range(0, LANES, 16):
            onehot[h * LANES + at : h * LANES + at + 16, :] = low_hot[at : at + 16, :] * row
    data = jnp.concatenate([block[g, :rows, :] for g in range(group)], axis=0)
    acc[...] += jnp.dot(onehot[...], data, preferred_element_type=F32)
    counts[...] += lax.dot_general(
        low_hot, high_hot.astype(BF16), (((1,), (1,)), ((), ())), preferred_element_type=F32
    )


def first_sums_body(group, rows, digits, block, acc, counts, onehot):
    @pl.when(pl.program_id(0) == 0)
    def _():
        acc[...] = jnp.zeros_like(acc)
        counts[...] = jnp.zeros_like(counts)

    accumulate(block, group, rows, digits, acc, counts, onehot)


def first_sums(arrived, rows, group, fine_dev):
    peers, tall, width = arrived.shape
    digits = fine_dev // LANES
    return pl.pallas_call(
        functools.partial(first_sums_body, group, rows, digits),
        grid=(peers // group,),
        out_shape=(
            jax.ShapeDtypeStruct((fine_dev, width), F32),
            jax.ShapeDtypeStruct((LANES, digits), F32),
        ),
        in_specs=[pl.BlockSpec((group, tall, width), lambda i: (i, 0, 0))],
        out_specs=(
            pl.BlockSpec((fine_dev, width), lambda i: (0, 0)),
            pl.BlockSpec((LANES, digits), lambda i: (0, 0)),
        ),
        scratch_shapes=[pltpu.VMEM((fine_dev, group * rows), BF16)],
        cost_estimate=pl.CostEstimate(
            flops=2 * peers * rows * fine_dev * width,
            bytes_accessed=arrived.size * 2 + fine_dev * width * 4,
            transcendentals=0,
        ),
        name="first_sums",
    )(arrived)


def last_sums_body(
    group, rows, digits, block, acc_in, counts_in, old, new, acc, counts, onehot
):
    @pl.when(pl.program_id(0) == 0)
    def _():
        acc[...] = acc_in[...]
        counts[...] = counts_in[...]

    accumulate(block, group, rows, digits, acc, counts, onehot)

    @pl.when(pl.program_id(0) == pl.num_programs(0) - 1)
    def _():
        for h in range(digits):
            at = slice(h * LANES, (h + 1) * LANES)
            total = acc[at, :] + old[at, :].astype(F32)
            new[at, :] = (total / (counts[:, h : h + 1] + 1.0)).astype(BF16)


def last_sums(arrived, acc, counts, old_fine, rows, group):
    peers, tall, width = arrived.shape
    fine_dev = old_fine.shape[0]
    digits = fine_dev // LANES
    whole = lambda a: pl.BlockSpec(a.shape, lambda i: (0, 0))
    return pl.pallas_call(
        functools.partial(last_sums_body, group, rows, digits),
        grid=(peers // group,),
        out_shape=jax.ShapeDtypeStruct((fine_dev, width), BF16),
        in_specs=[
            pl.BlockSpec((group, tall, width), lambda i: (i, 0, 0)),
            whole(acc),
            whole(counts),
            whole(old_fine),
        ],
        out_specs=pl.BlockSpec((fine_dev, width), lambda i: (0, 0)),
        scratch_shapes=[
            pltpu.VMEM((fine_dev, width), F32),
            pltpu.VMEM((LANES, digits), F32),
            pltpu.VMEM((fine_dev, group * rows), BF16),
        ],
        name="last_sums",
    )(arrived, acc, counts, old_fine)


def plan_body(coarse_dev, ids, owner_hot, rank_hot, labels):
    peers, fine_dev = owner_hot.shape
    value = ids[...]
    owner = value // coarse_dev
    local = (value - owner * coarse_dev).astype(F32)
    member = jnp.where(iota((peers, fine_dev), 0) == owner, 1.0, 0.0)
    owner_hot[...] = member
    step = 256
    before = jnp.where(iota((step, step), 0) < iota((step, step), 1), 1.0, 0.0).astype(BF16)
    carry = jnp.zeros((peers, 1), F32)
    for at in range(0, fine_dev, step):
        piece = member[:, at : at + step]
        prefix = jnp.dot(piece.astype(BF16), before, preferred_element_type=F32) + carry
        rank = jnp.sum(prefix * piece, axis=0, keepdims=True)
        carry = carry + jnp.sum(piece, axis=1, keepdims=True)
        hot = jnp.where(iota((rank_hot.shape[0], step), 0).astype(F32) == rank, 1.0, 0.0)
        rank_hot[:, at : at + step] = hot.astype(BF16)
    tagged = (member * (local + 1.0)).astype(BF16)
    labels[...] = lax.dot_general(
        tagged, rank_hot[...], (((1,), (1,)), ((), ())), preferred_element_type=F32
    )


def plan(coarse_ids, peers, capacity, coarse_dev):
    fine_dev = coarse_ids.shape[1]
    return pl.pallas_call(
        functools.partial(plan_body, coarse_dev),
        out_shape=(
            jax.ShapeDtypeStruct((peers, fine_dev), F32),
            jax.ShapeDtypeStruct((capacity, fine_dev), BF16),
            jax.ShapeDtypeStruct((peers, capacity), F32),
        ),
        name="plan_clusters",
    )(coarse_ids)


def place_body(group, owner_hot, rank_hot, new, out, placement):
    capacity, fine_dev = rank_hot.shape
    for g in range(group):
        row = jnp.broadcast_to(owner_hot[g : g + 1, :], (16, fine_dev)).astype(BF16)
        for at in range(0, capacity, 16):
            top = g * capacity + at
            placement[top : top + 16, :] = rank_hot[at : at + 16, :] * row
    sent = jnp.dot(placement[...], new[...], preferred_element_type=F32).astype(BF16)
    for g in range(group):
        out[g, :, :] = sent[g * capacity : (g + 1) * capacity, :]


def place(owner_hot, rank_hot, new_fine, group):
    peers, fine_dev = owner_hot.shape
    capacity = rank_hot.shape[0]
    width = new_fine.shape[1]
    whole = lambda a: pl.BlockSpec(a.shape, lambda i: (0, 0))
    return pl.pallas_call(
        functools.partial(place_body, group),
        grid=(peers // group,),
        out_shape=jax.ShapeDtypeStruct((peers, capacity, width), BF16),
        in_specs=[
            pl.BlockSpec((group, fine_dev), lambda i: (i, 0)),
            whole(rank_hot),
            whole(new_fine),
        ],
        out_specs=pl.BlockSpec((group, capacity, width), lambda i: (i, 0, 0)),
        scratch_shapes=[pltpu.VMEM((group * capacity, fine_dev), BF16)],
        name="place_clusters",
    )(owner_hot, rank_hot, new_fine)


def coarse_body(received, tags, old, means, onehot):
    peers, capacity, width = received.shape
    coarse_dev = old.shape[0]
    total = jnp.zeros((coarse_dev, capacity), F32)
    row = iota((coarse_dev, capacity), 0).astype(F32) + 1.0
    for p in range(peers):
        hot = jnp.where(row == tags[p, 1:2, :capacity].astype(F32), 1.0, 0.0)
        total = total + hot
        onehot[:, p * capacity : (p + 1) * capacity] = hot.astype(BF16)
    data = received[...].reshape(peers * capacity, width)
    sums = jnp.dot(onehot[...], data, preferred_element_type=F32)
    count = jnp.sum(total, axis=1, keepdims=True)
    means[...] = ((sums + old[...].astype(F32)) / (count + 1.0)).astype(BF16)


def coarse(received, arrived_tail, rows, old_coarse):
    peers, capacity, width = received.shape
    return pl.pallas_call(
        coarse_body,
        grid=(1,),
        out_shape=jax.ShapeDtypeStruct(old_coarse.shape, BF16),
        in_specs=[
            pl.BlockSpec(received.shape, lambda i: (0, 0, 0)),
            pl.BlockSpec((peers, TAIL, width), lambda i: (0, rows // TAIL, 0)),
            pl.BlockSpec(old_coarse.shape, lambda i: (0, 0)),
        ],
        out_specs=pl.BlockSpec(old_coarse.shape, lambda i: (0, 0)),
        scratch_shapes=[pltpu.VMEM((old_coarse.shape[0], peers * capacity), BF16)],
        name="coarse_means",
    )(received, arrived_tail, old_coarse)


def finish_body(groups, at, *refs):
    pieces, out, full = refs[:groups], refs[groups], refs[groups + 1]
    width = pieces[0].shape[1]
    for step in range(groups):
        place = lax.rem(at[0] + step, groups) * width
        full[:, pl.ds(pl.multiple_of(place, width), width)] = pieces[step][...].astype(F32)
    whole = full[...]
    scale = lax.rsqrt(jnp.mean(whole * whole, axis=1, keepdims=True) + 1e-06)
    out[...] = (whole * scale).astype(BF16)


def finish(at, pieces):
    groups = len(pieces)
    rows, width = pieces[0].shape
    return pl.pallas_call(
        functools.partial(finish_body, groups),
        out_shape=jax.ShapeDtypeStruct((rows, groups * width), BF16),
        in_specs=[pl.BlockSpec(memory_space=pltpu.SMEM)]
        + [pl.BlockSpec(memory_space=pltpu.VMEM)] * groups,
        scratch_shapes=[pltpu.VMEM((rows, groups * width), F32)],
        name="coarse_dirs",
    )(at, *pieces)


def exchange(slots):
    return lax.all_to_all(slots, "rows", split_axis=0, concat_axis=0, tiled=True)


def on_device(embeddings, fine_local, send_counts, old_fine, coarse_ids, old_coarse):
    peers = lax.axis_size("rows")
    groups = lax.axis_size("grp")
    per_dev = embeddings.shape[0]
    fine_dev = old_fine.shape[0]
    coarse_dev = old_coarse.shape[0]
    capacity = 2 * per_dev // peers
    capacity_two = 2 * fine_dev // peers
    second = capacity - FIRST
    local = fine_local.reshape(-1, LANES)

    slots = pack(send_counts, embeddings, local, None, 0, FIRST, capacity)
    arrived = exchange(slots)
    owner_hot, rank_hot, tags = plan(
        coarse_ids.reshape(1, -1), peers, capacity_two, coarse_dev
    )
    more_slots = pack(send_counts, embeddings, local, tags, FIRST, second, capacity)
    more = exchange(more_slots)

    acc, counts = first_sums(arrived, FIRST, 2, fine_dev)
    new_fine = last_sums(more, acc, counts, old_fine, second, 4)

    received = exchange(place(owner_hot, rank_hot, new_fine, 8))
    means = coarse(received, more, second, old_coarse)
    pieces = [means]
    for step in range(1, groups):
        back = [((g + step) % groups, g) for g in range(groups)]
        pieces.append(lax.ppermute(means, "grp", back))
    at = lax.axis_index("grp").astype(jnp.int32).reshape(1)
    return (new_fine, finish(at, pieces))


def solution(mesh):
    in_specs = (
        P("rows", "grp"),
        P("rows"),
        P("rows", None),
        P("rows", "grp"),
        P("rows"),
        P("rows", "grp"),
    )
    out_specs = (P("rows", "grp"), P("rows", None))
    return jax.shard_map(
        on_device, mesh=mesh, in_specs=in_specs, out_specs=out_specs, check_vma=False
    )
```

time: 450 us -> 223 us (0.50)
  local copies, waits for them, and re-layouts: 87.8 us -> 2.04 us
  Pallas kernels: 0 us -> 77.6 us
  loops' own time: 67.7 us -> 0 us
  waiting for transfers between devices: 148 us -> 84 us
  matrix products: 54.3 us -> 0 us
  other arithmetic: 37.7 us -> 0 us
  blocking collectives: 0 us -> 32.7 us
  between operations: 14.2 us -> 0.66 us
  starting transfers between devices: 36.7 us -> 24.2 us
    pallas_call x0 -> x8, Pallas kernels: none -> 77.6 us  [the longest x2 33 us: pack(): pl.pallas_call(functools.partial(pack_body, lo_row, rows, capacity), grid...]
    another operation x2 -> x0, loops' own time: 67.7 us -> none  [the longest x1 67.3 us: on_device(): outgoing, raw_labels = lax.map(take_segment, starts)]
    dynamic_update_slice x64 -> x0, local copies, waits for them, and re-layouts: 56.5 us -> none  [on_device(): outgoing, raw_labels = lax.map(take_segment, starts)]
    dot_general x11 -> x0, matrix products: 54.3 us -> none  [the longest x8 39.8 us: accumulate(): jnp.dot(onehot.astype(jnp.bfloat16), row_block, preferred_element_type=jn...]
    all_to_all x4 -> x2, waiting for transfers between devices: 125 us -> 75.5 us  [exchange(): lax.all_to_all(slots, 'rows', split_axis=0, concat_axis=0, tiled=True)]
    all_to_all x0 -> x1, blocking collectives: none -> 32.7 us  [exchange(): lax.all_to_all(slots, 'rows', split_axis=0, concat_axis=0, tiled=True)]
    dynamic_slice x72 -> x0, local copies, waits for them, and re-layouts: 23.9 us -> none  [the longest x32 21.4 us: on_device(): outgoing, raw_labels = lax.map(take_segment, starts)]
    all_gather x1 -> x0, waiting for transfers between devices: 22.8 us -> none  [on_device(): full_means = lax.all_gather(coarse_means, 'grp', axis=1, tiled=True)]
  transfers between devices with their start and end apart: 5 -> 5, of which waited for: 3 -> 5; matrix products, arithmetic and copies ran while one was open for 19% -> 0% of each run, Pallas kernels for 0% -> 17%
where the time goes in v1:
time: 223 us; the launch traced here: 221 us
  waiting for transfers between devices  84 us (38%)
  Pallas kernels  77.6 us (35%)
  blocking collectives  32.7 us (15%)
  starting transfers between devices  24.2 us (11%)
    all_to_all x2, waiting for transfers between devices, exchange(): lax.all_to_all(slots, 'rows', split_axis=0, concat_axis=0, tiled=True)  75.5 us
    pallas_call x2, Pallas kernels, pack(): pl.pallas_call(functools.partial(pack_body, lo_row, rows, capacity), grid...  33 us
    all_to_all x1, blocking collectives, exchange(): lax.all_to_all(slots, 'rows', split_axis=0, concat_axis=0, tiled=True)  32.7 us
    pallas_call x1, Pallas kernels, first_sums(): pl.pallas_call(functools.partial(first_sums_body, group, rows, digits), g...  19.5 us
    all_to_all x2, starting transfers between devices, exchange(): lax.all_to_all(slots, 'rows', split_axis=0, concat_axis=0, tiled=True)  19 us
    pallas_call x1, Pallas kernels, last_sums(): pl.pallas_call(functools.partial(last_sums_body, group, rows, digits), gr...  10.2 us
    ppermute x3, waiting for transfers between devices, on_device(): pieces.append(lax.ppermute(means, 'grp', back))  8.51 us
    pallas_call x1, Pallas kernels, place(): pl.pallas_call(functools.partial(place_body, group), grid=(peers // group...  7.29 us
  transfers between devices with their start and end apart: 5, of which 5 were waited for; matrix products, arithmetic and copies ran while one was open for 0% of the time, Pallas kernels for 17%

profile of v1, /device:TPU:0, one launch (start us, length us, event | category | flops | bytes accessed | tf_op | source)
XLA Modules:
  0.0 221.3 jit_solution(9936233750189936960)
XLA Ops:
  0.6 16.9 %pack_rows.3 = bf16[32,392,256]{2,1,0:T(8,128)(2,1)} custom-call(s32[1,32]{1,0:T(1,128)} %counts.3, bf16[8192,256]{1,0:T(8,128)(2,1)} %emb.3, s32[64,128]{1,0:T(8,128)} %bitcast.3), custom_call_target="tpu_custom_call" | custom-call | tf_op jit(solution)/shard_map/pack_rows/pallas_call | solution.py:74
  17.6 7.5 %all-to-all-start.1 = ((bf16[32,392,256]{2,1,0:T(8,128)(2,1)}), bf16[32,392,256]{2,1,0:T(8,128)(2,1)}, u32[]{:S(2)}, u32[]{:S(2)}) async-start(bf16[32,392,256]{2,1,0:T(8,128)(2,1)} %pack_rows.3), calls=%async_computation.1 | async-start | bytes 12845056 | tf_op jit(solution)/shard_map/all_to_all | solution.py:313
  25.1 1.9 plan_clusters.1
  27.1 16.0 %pack_rows.2 = bf16[32,136,256]{2,1,0:T(8,128)(2,1)} custom-call(s32[1,32]{1,0:T(1,128)} %counts.3, bf16[8192,256]{1,0:T(8,128)(2,1)} %emb.3, s32[64,128]{1,0:T(8,128)} %bitcast.4, f32[32,128]{1,0:T(8,128)} %get-tuple-element.7.rest_0_), custom_call_target="tpu_custom_call" | custom-call | tf_op jit(solution)/shard_map/pack_rows/pallas_call | solution.py:74
  43.1 64.6 %all-to-all-done.1.block = bf16[32,392,256]{2,1,0:T(8,128)(2,1)} async-done(((bf16[32,392,256]{2,1,0:T(8,128)(2,1)}), bf16[32,392,256]{2,1,0:T(8,128)(2,1)}, u32[]{:S(2)}, u32[]{:S(2)}) %all-to-all-start.1) | async-done | bytes 6422560 | tf_op jit(solution)/shard_map/all_to_all | solution.py:313
  107.7 11.4 %all-to-all-start = ((bf16[32,136,256]{2,1,0:T(8,128)(2,1)}), bf16[32,136,256]{2,1,0:T(8,128)(2,1)S(1)}, u32[]{:S(2)}, u32[]{:S(2)}) async-start(bf16[32,136,256]{2,1,0:T(8,128)(2,1)} %pack_rows.2), calls=%async_computation | async-start | bytes 4456448 | tf_op jit(solution)/shard_map/all_to_all | solution.py:313
  119.1 19.5 %first_sums.1 = (f32[2048,256]{1,0:T(8,128)}, f32[128,16]{1,0:T(8,128)}) custom-call(bf16[32,392,256]{2,1,0:T(8,128)(2,1)} %all-to-all-done.1.block), custom_call_target="tpu_custom_call" | custom-call | flops 12884901888 | bytes 8519680 | tf_op jit(solution)/shard_map/first_sums/pallas_call | solution.py:123
  138.6 10.9 %all-to-all-done.block.tags = bf16[32,136,256]{2,1,0:T(8,128)(2,1)S(1)} async-done(((bf16[32,136,256]{2,1,0:T(8,128)(2,1)}), bf16[32,136,256]{2,1,0:T(8,128)(2,1)S(1)}, u32[]{:S(2)}, u32[]{:S(2)}) %all-to-all-start) | async-done | bytes 2228256 | tf_op jit(solution)/shard_map/all_to_all | solution.py:313
  149.5 0.0 copy-start
  149.5 1.4 copy-done
  150.9 10.2 %last_sums.1.new = bf16[2048,256]{1,0:T(8,128)(2,1)} custom-call(bf16[32,136,256]{2,1,0:T(8,128)(2,1)} %copy-done, f32[2048,256]{1,0:T(8,128)} %get-tuple-element.8.acc_in, f32[128,16]{1,0:T(8,128)} %get-tuple-element.9.counts_in, bf16[2048,256]{1,0:T(8,128)(2,1)} %old.2), custom_call_target="tpu_custom_call" | custom-call | tf_op jit(solution)/shard_map/last_sums/pallas_call | solution.py:168
  161.1 7.3 %place_clusters.1 = bf16[32,128,256]{2,1,0:T(8,128)(2,1)} custom-call(f32[32,2048]{1,0:T(8,128)} %get-tuple-element.10.owner_hot, bf16[128,2048]{1,0:T(8,128)(2,1)} %get-tuple-element.11.rank_hot, bf16[2048,256]{1,0:T(8,128)(2,1)} %last_sums.1.new), custom_call_target="tpu_custom_call" | custom-call | tf_op jit(solution)/shard_map/place_clusters/pallas_call | solution.py:241
  168.4 32.7 %all_to_all.15.received = bf16[32,128,256]{2,1,0:T(8,128)(2,1)} all-to-all(bf16[32,128,256]{2,1,0:T(8,128)(2,1)} %place_clusters.1), channel_id=1, replica_groups=mesh['rows'=32,'grp'=4] {'rows'}, dimensions={0} | all-to-all | bytes 4194304 | tf_op jit(solution)/shard_map/all_to_all | solution.py:313
  201.1 3.5 %coarse_means.1.refs_0_ = bf16[256,256]{1,0:T(8,128)(2,1)} custom-call(bf16[32,128,256]{2,1,0:T(8,128)(2,1)} %all_to_all.15.received, bf16[32,136,256]{2,1,0:T(8,128)(2,1)} %copy-done, bf16[256,256]{1,0:T(8,128)(2,1)} %old.3), custom_call_target="tpu_custom_call" | custom-call | tf_op jit(solution)/shard_map/coarse_means/pallas_call | solution.py:273
  204.7 4.0 %collective-permute-start = (bf16[256,256]{1,0:T(8,128)(2,1)}, bf16[256,256]{1,0:T(8,128)(2,1)S(1)}, u32[]{:S(2)}, u32[]{:S(2)}) collective-permute-start(bf16[256,256]{1,0:T(8,128)(2,1)} %coarse_means.1.refs_0_), channel_id=1, source_target_pairs={{1,0},{2,1},{3,2},{0,3},{5,4},{6,5},{7,6},{4,7},{9,8},{10,9},{11,1... | collective-permute-start | bytes 393224 | tf_op jit(solution)/shard_map/ppermute | solution.py:343
  208.7 0.0 collective-permute-start.1
  208.7 1.2 collective-permute-start.2
  209.9 5.2 %collective-permute-done.refs_1_ = bf16[256,256]{1,0:T(8,128)(2,1)S(1)} collective-permute-done((bf16[256,256]{1,0:T(8,128)(2,1)}, bf16[256,256]{1,0:T(8,128)(2,1)S(1)}, u32[]{:S(2)}, u32[]{:S(2)}) %collective-permute-start) | collective-permute-done | bytes 131104 | tf_op jit(solution)/shard_map/ppermute | solution.py:343
  215.1 1.7 collective-permute-done.1.refs_2_
  216.8 1.6 collective-permute-done.2.refs_3_
  218.4 0.0 copy-done.1
  218.5 0.0 copy-done.2
  218.5 0.7 copy-done.3
  219.1 2.2 coarse_dirs.1
  (3 shorter events, 0.0 us)
Async XLA Ops:
  17.6 90.2 %all-to-all-start.1 = ((bf16[32,392,256]{2,1,0:T(8,128)(2,1)}), bf16[32,392,256]{2,1,0:T(8,128)(2,1)}, u32[]{:S(2)}, u32[]{:S(2)}) async-start(bf16[32,392,256]{2,1,0:T(8,128)(2,1)} %pack_rows.3), calls=%async_computation.1 | async-start | bytes 12845056 | tf_op jit(solution)/shard_map/all_to_all | solution.py:313
  107.7 41.8 %all-to-all-start = ((bf16[32,136,256]{2,1,0:T(8,128)(2,1)}), bf16[32,136,256]{2,1,0:T(8,128)(2,1)S(1)}, u32[]{:S(2)}, u32[]{:S(2)}) async-start(bf16[32,136,256]{2,1,0:T(8,128)(2,1)} %pack_rows.2), calls=%async_computation | async-start | bytes 4456448 | tf_op jit(solution)/shard_map/all_to_all | solution.py:313
  149.5 1.4 copy-start
  204.7 10.5 %collective-permute-start = (bf16[256,256]{1,0:T(8,128)(2,1)}, bf16[256,256]{1,0:T(8,128)(2,1)S(1)}, u32[]{:S(2)}, u32[]{:S(2)}) collective-permute-start(bf16[256,256]{1,0:T(8,128)(2,1)} %coarse_means.1.refs_0_), channel_id=1, source_target_pairs={{1,0},{2,1},{3,2},{0,3},{5,4},{6,5},{7,6},{4,7},{9,8},{10,9},{11,1... | collective-permute-start | bytes 393224 | tf_op jit(solution)/shard_map/ppermute | solution.py:343
  208.7 8.1 %collective-permute-start.1 = (bf16[256,256]{1,0:T(8,128)(2,1)}, bf16[256,256]{1,0:T(8,128)(2,1)S(1)}, u32[]{:S(2)}, u32[]{:S(2)}) collective-permute-start(bf16[256,256]{1,0:T(8,128)(2,1)} %coarse_means.1.refs_0_), channel_id=1, source_target_pairs={{2,0},{3,1},{0,2},{1,3},{6,4},{7,5},{4,6},{5,7},{10,8},{11,9},{8,1... | collective-permute-start | bytes 393224 | tf_op jit(solution)/shard_map/ppermute | solution.py:343
  208.7 9.7 %collective-permute-start.2 = (bf16[256,256]{1,0:T(8,128)(2,1)}, bf16[256,256]{1,0:T(8,128)(2,1)S(1)}, u32[]{:S(2)}, u32[]{:S(2)}) collective-permute-start(bf16[256,256]{1,0:T(8,128)(2,1)} %coarse_means.1.refs_0_), channel_id=1, source_target_pairs={{3,0},{0,1},{1,2},{2,3},{7,4},{4,5},{5,6},{6,7},{11,8},{8,9},{9,10... | collective-permute-start | bytes 393224 | tf_op jit(solution)/shard_map/ppermute | solution.py:343
  215.1 3.3 %copy-start.1 = (bf16[256,256]{1,0:T(8,128)(2,1)}, bf16[256,256]{1,0:T(8,128)(2,1)S(1)}, u32[]{:S(2)}) copy-start(bf16[256,256]{1,0:T(8,128)(2,1)S(1)} %collective-permute-done.refs_1_) | copy-start | bytes 393220
  216.8 1.6 copy-start.2
  218.4 0.7 copy-start.3
